TPU v7x, 128 devices: a whole 4x4x4 slice. The times are simulated.
128 devices in a mesh: seq: 8 (over x, core), grp: 16 (over z, y).
Axes of the slice: x: 4, y: 4, z: 4, core: 2. Of those that a mesh axis runs over, the one named last changes fastest.
Arguments:
- tokens: bfloat16 [16, 1024, 1536], P('grp', 'seq'), may hold values from -15 to 15
- lengths: int32 [16, 3], P('grp'), may hold values from 1 to 512, 1024 in all within a row
- prompt_adapter: int32 [16, 3], P('grp'), may hold values from 0 to 15
- routes: int32 [16, 1024, 8], P('grp', 'seq'), may hold values from 0 to 39, all different within a row; in each aligned block of 128 rows (0 to 127, 128 to 255, ..., all dimensions but the last counted through in order) at most 40 rows name the same one
- routing_weight: float32 [16, 1024, 8], P('grp', 'seq'), may hold values from 0.1 to 1
- attention_gain: float32 [1536], replicated, may hold values from 0.5 to 1.5
- query_weight: bfloat16 [1536, 1536], replicated, may hold values from -25 to 25
- key_weight: bfloat16 [1536, 512], replicated, may hold values from -0.15625 to 0.15625
- value_weight: bfloat16 [1536, 512], replicated, may hold values from -0.15625 to 0.15625
- output_weight: bfloat16 [1536, 1536], replicated, may hold values from -0.15625 to 0.15625
- adapter_down_maps: bfloat16 [4, 16, 1536, 16], P(None, 'grp'), may hold values from -0.15625 to 0.15625
- adapter_up_query_output: bfloat16 [2, 16, 16, 1536], P(None, 'grp'), may hold values from -1.5 to 1.5
- adapter_up_key_value: bfloat16 [2, 16, 16, 512], P(None, 'grp'), may hold values from -1.5 to 1.5
- expert_gain: float32 [1536], replicated, may hold values from 0.5 to 1.5
- gate_weight: bfloat16 [80, 1536, 256], P('grp'), may hold values from -0.15625 to 0.15625
- up_weight: bfloat16 [80, 1536, 256], P('grp'), may hold values from -0.15625 to 0.15625
- down_weight: bfloat16 [80, 256, 1536], P('grp'), may hold values from -0.25 to 0.25
- closing_gain: float32 [1536], replicated, may hold values from 0.5 to 1.5
- vocab_projection: bfloat16 [1536, 49152], P(None, ('seq', 'grp')), may hold values from -10 to 10
Outputs:
- hidden_out: bfloat16 [16, 1024, 1536], P('grp', 'seq')
- log_probs: float32 [48, 49152], P(None, ('seq', 'grp'))
Inputs may be any that keep to these rules, and one draw needn't show every extreme that they name: The 3 lengths of a group sum to 1024; the longest is exactly 512. `routes`: A token names 8 different experts. Within the 128 tokens of one device no expert is named by more than 40 of them, and in every draw some expert is named by exactly 40 tokens of some device.
All inputs are finite; a program needn't handle non-finite values.
Results may differ from a plain program's by a relative error of at most 0.017.
The roundings to bfloat16 on the way count: a program that leaves them out, or rounds other values in their place, can miss the bound.
Values may be sent and summed in bfloat16 or wider, within the bound.
No kernel may reach another device: no remote copies, remote signals or barrier semaphores. Data moves between devices by JAX's collectives and lax.ppermute only.
A program may use at most 192 MiB of HBM per device.

v0:
```python
import jax
import jax.numpy as jnp
from jax import lax
from jax.sharding import PartitionSpec as P

HEADS = 24
KV_HEADS = 8
HEAD = 64
EXPERTS = 40
TOP = 8
CAP = 40
EPSILON = 1e-05
ROPE_BASE = 10000.0
MASKED = -1e30


def rms_scaled(features, scales):
    features = features.astype(jnp.float32)
    inverse = lax.rsqrt(jnp.mean(features * features, axis=-1, keepdims=True) + EPSILON)
    return (features * inverse * scales).astype(jnp.bfloat16)


def rotate(features, offsets):
    half_size = features.shape[-1] // 2
    frequency = ROPE_BASE ** (-jnp.arange(half_size, dtype=jnp.float32) / half_size)
    angles = offsets.astype(jnp.float32)[:, None, None] * frequency[None, None, :]
    cosine = jnp.cos(angles)
    sines = jnp.sin(angles)
    first_half = features[..., :half_size]
    second = features[..., half_size:]
    return jnp.concatenate(
        [first_half * cosine - second * sines, second * cosine + first_half * sines], axis=-1
    )


def doc_layout(prompt_lens, row_index):
    doc_ends = jnp.cumsum(prompt_lens)
    starts = doc_ends - prompt_lens
    document = jnp.sum((row_index[:, None] >= doc_ends[None, :]).astype(jnp.int32), axis=1)
    member = document[:, None] == jnp.arange(prompt_lens.shape[0], dtype=jnp.int32)[None, :]
    doc_start = jnp.sum(jnp.where(member, starts[None, :], 0), axis=1)
    return (document, row_index - doc_start, member)


def adapter_delta(normalized_rows, selected_experts, down_proj, up_weights):
    low_rank = jnp.einsum(
        "td,adr->tar", normalized_rows, down_proj, preferred_element_type=jnp.float32
    )
    low_rank = (low_rank * selected_experts[:, :, None]).astype(jnp.bfloat16)
    return jnp.einsum("tar,are->te", low_rank, up_weights, preferred_element_type=jnp.float32)


def body(
    tokens,
    lengths,
    prompt_adapter,
    routes,
    routing_weight,
    attention_gain,
    query_weight,
    key_weight,
    value_weight,
    output_weight,
    adapter_down_maps,
    adapter_up_query_output,
    adapter_up_key_value,
    expert_gain,
    gate_weight,
    up_weight,
    down_weight,
    closing_gain,
    vocab_projection,
):
    rows_in = tokens[0]
    tok_count = rows_in.shape[0]
    model_width = rows_in.shape[1]
    prompt_lens = lengths[0]
    owners = prompt_adapter[0]
    ratio = HEADS // KV_HEADS
    logit_scale = HEAD ** (-0.5)
    down_all, wide_all, narrow_all = (
        lax.all_gather(adapter_down_maps, "grp", axis=1, tiled=True),
        lax.all_gather(adapter_up_query_output, "grp", axis=1, tiled=True),
        lax.all_gather(adapter_up_key_value, "grp", axis=1, tiled=True),
    )
    row_index = lax.axis_index("seq") * tok_count + jnp.arange(tok_count, dtype=jnp.int32)
    document, offsets, member = doc_layout(prompt_lens, row_index)
    adapter = jnp.sum(jnp.where(member, owners[None, :], 0), axis=1)
    selected_experts = (
        adapter[:, None] == jnp.arange(down_all.shape[1], dtype=jnp.int32)[None, :]
    ).astype(jnp.float32)
    normalized_rows = rms_scaled(rows_in, attention_gain)
    query_matrix = jnp.dot(
        normalized_rows, query_weight, preferred_element_type=jnp.float32
    ) + adapter_delta(normalized_rows, selected_experts, down_all[0], wide_all[0])
    query_matrix = rotate(query_matrix.reshape(tok_count, HEADS, HEAD), offsets).astype(
        jnp.bfloat16
    )
    query_matrix = query_matrix.reshape(tok_count, KV_HEADS, ratio, HEAD)
    key_matrix = jnp.dot(
        normalized_rows, key_weight, preferred_element_type=jnp.float32
    ) + adapter_delta(normalized_rows, selected_experts, down_all[1], narrow_all[0])
    key_matrix = (
        rotate(key_matrix.reshape(tok_count, KV_HEADS, HEAD), offsets)
        .astype(jnp.bfloat16)
        .reshape(tok_count, KV_HEADS * HEAD)
    )
    value_matrix = (
        jnp.dot(normalized_rows, value_weight, preferred_element_type=jnp.float32)
        + adapter_delta(normalized_rows, selected_experts, down_all[2], narrow_all[1])
    ).astype(jnp.bfloat16)
    running_max = jnp.full((KV_HEADS, ratio, tok_count), MASKED, jnp.float32)
    key_part = lax.all_gather(key_matrix, "seq", axis=0, tiled=True)
    value_part = lax.all_gather(value_matrix, "seq", axis=0, tiled=True)
    key_count = key_part.shape[0]
    key_index = jnp.arange(key_count, dtype=jnp.int32)
    key_doc, _, _ = doc_layout(prompt_lens, key_index)
    allowed = (key_doc[None, :] == document[:, None]) & (key_index[None, :] <= row_index[:, None])
    attention_logits = (
        jnp.einsum(
            "jhlv,phv->hljp",
            query_matrix,
            key_part.reshape(key_count, KV_HEADS, HEAD),
            preferred_element_type=jnp.float32,
        )
        * logit_scale
    )
    attention_logits = jnp.where(allowed[None, None], attention_logits, MASKED)
    new_max = jnp.maximum(running_max, jnp.max(attention_logits, axis=-1))
    weights = jnp.where(allowed[None, None], jnp.exp(attention_logits - new_max[..., None]), 0.0)
    running_sum = jnp.sum(weights, axis=-1)
    weighted_values = jnp.einsum(
        "ukoe,euh->ukoh",
        weights.astype(jnp.bfloat16),
        value_part.reshape(key_count, KV_HEADS, HEAD),
        preferred_element_type=jnp.float32,
    )
    running_max, running_sum, weighted_values = (new_max, running_sum, weighted_values)
    attention_output = (
        (weighted_values / running_sum[..., None])
        .transpose(2, 0, 1, 3)
        .reshape(tok_count, HEADS * HEAD)
        .astype(jnp.bfloat16)
    )
    outside_mask = jnp.dot(
        attention_output, output_weight, preferred_element_type=jnp.float32
    ) + adapter_delta(attention_output, selected_experts, down_all[3], wide_all[1])
    mixed_rows = (rows_in.astype(jnp.float32) + outside_mask).astype(jnp.bfloat16)
    moe_in = rms_scaled(mixed_rows, expert_gain)
    expert_ids = routes[0].reshape(-1)
    flat_weights = routing_weight[0].reshape(-1)
    onehot = (expert_ids[:, None] == jnp.arange(EXPERTS, dtype=jnp.int32)[None, :]).astype(
        jnp.int32
    )
    slot_index = jnp.sum((jnp.cumsum(onehot, axis=0) - onehot) * onehot, axis=1)
    source_row = jnp.arange(expert_ids.shape[0], dtype=jnp.int32) // TOP
    slot_table = (
        jnp.full((EXPERTS * CAP,), tok_count, jnp.int32)
        .at[expert_ids * CAP + slot_index]
        .set(source_row)
        .reshape(EXPERTS, CAP)
    )
    padded = jnp.concatenate([moe_in, jnp.zeros((1, model_width), jnp.bfloat16)], axis=0)
    groups = lax.axis_size("grp")
    slices_here = gate_weight.shape[0]
    outgoing = padded[jnp.repeat(slot_table, 2, axis=0)].reshape(
        groups, slices_here, CAP, model_width
    )
    arrived = lax.all_to_all(outgoing, "grp", split_axis=0, concat_axis=0, tiled=True)
    gate_proj = jnp.einsum(
        "nlcd,ldf->nlcf", arrived, gate_weight, preferred_element_type=jnp.float32
    )
    up_proj = jnp.einsum("nlcd,ldf->nlcf", arrived, up_weight, preferred_element_type=jnp.float32)
    hidden = (jax.nn.silu(gate_proj) * up_proj).astype(jnp.bfloat16)
    halves = jnp.einsum(
        "nlcf,lfd->nlcd", hidden, down_weight, preferred_element_type=jnp.float32
    ).astype(jnp.bfloat16)
    returned = lax.all_to_all(halves, "grp", split_axis=0, concat_axis=0, tiled=True).reshape(
        -1, model_width
    )
    slice_ids = 2 * expert_ids[:, None] + jnp.arange(2, dtype=jnp.int32)[None, :]
    pick_index = slice_ids * CAP + slot_index[:, None]
    picked = returned[pick_index].astype(jnp.float32).reshape(tok_count, TOP * 2, model_width)
    holder = slice_ids // slices_here
    holder_hot = (holder[:, :, None] == jnp.arange(groups, dtype=jnp.int32)[None, None, :]).astype(
        jnp.float32
    )
    holder_hot = (holder_hot * flat_weights[:, None, None]).reshape(tok_count, TOP * 2, groups)
    partial_value = jnp.einsum(
        "tkg,tkd->tgd", holder_hot, picked, precision=lax.Precision.HIGHEST
    ).astype(jnp.bfloat16)
    combined = jnp.sum(partial_value.astype(jnp.float32), axis=1)
    hidden_out = (mixed_rows.astype(jnp.float32) + combined).astype(jnp.bfloat16)
    last_index = jnp.cumsum(prompt_lens) - 1
    selector = (last_index[:, None] == row_index[None, :]).astype(jnp.bfloat16)
    last_rows = jnp.dot(selector, hidden_out, preferred_element_type=jnp.float32)
    last_rows = rms_scaled(last_rows, closing_gain).astype(jnp.float32)
    own_group = (jnp.arange(groups, dtype=jnp.int32) == lax.axis_index("grp")).astype(jnp.float32)
    spread = own_group[:, None, None] * last_rows[None, :, :]
    gathered = lax.psum(spread, ("seq", "grp"))
    final_rows = gathered.reshape(-1, model_width).astype(jnp.bfloat16)
    logits = jnp.dot(final_rows, vocab_projection, preferred_element_type=jnp.float32)
    global_max = lax.pmax(jnp.max(logits, axis=1), ("seq", "grp"))
    global_sum = lax.psum(jnp.sum(jnp.exp(logits - global_max[:, None]), axis=1), ("seq", "grp"))
    log_probs = logits - (global_max + jnp.log(global_sum))[:, None]
    return (hidden_out[None], log_probs)


def solution(mesh):
    placed = (
        P("grp", "seq", None),
        P("grp", None),
        P("grp", None),
        P("grp", "seq", None),
        P("grp", "seq", None),
        P(),
        P(),
        P(),
        P(),
        P(),
        P(None, "grp", None, None),
        P(None, "grp", None, None),
        P(None, "grp", None, None),
        P(),
        P("grp", None, None),
        P("grp", None, None),
        P("grp", None, None),
        P(),
        P(None, ("seq", "grp")),
    )
    return jax.shard_map(
        body,
        mesh=mesh,
        in_specs=placed,
        out_specs=(P("grp", "seq", None), P(None, ("seq", "grp"))),
        check_vma=False,
    )
```

profile of v0, /device:TPU:1, one launch (start us, length us, event | category | flops | bytes accessed | tf_op | source)
XLA Modules:
  0.0 710.5 jit_solution(9158568903717004309)
XLA Ops:
  7.2 0.7 all-gather.5.cloned.1.call-update
  8.0 0.7 all-gather.9.cloned.1.call-update
  8.7 0.8 copy.64
  9.7 0.7 multiply_bitcast_fusion
  10.4 0.8 reduce-window.10
  11.2 0.7 fusion.77
  12.1 22.3 %all_gather.16 = bf16[2,16,16,512]{3,2,1,0:T(8,128)(2,1)S(1)} all-gather(bf16[2,1,16,512]{3,2,1,0:T(8,128)(2,1)} %param.31), channel_id=1, replica_groups=mesh['seq'=8,'grp'=16] {'grp'}, dimensions={1}, use_global_device_ids=true | all-gather | bytes 557056 | tf_op jit(solution)/shard_map/all_gather | solution.py:84
  34.4 11.3 %reduce-window.11 = s32[40,8,128]{2,1,0:T(8,128)S(1)} reduce-window(s32[40,8,128]{2,1,0:T(8,128)S(1)} %fusion.60, s32[]{:T(128)} %constant.32.clone.1), window={size=1x1x128 pad=0_0x0_0x127_0}, to_apply=%region_9.10 | reduce-window | flops 5201920 | bytes 327684 | tf_op jit(solution)/shard_map/reduce-window.1
  46.4 4.3 scatter_custom_fusion
  50.9 0.7 select_reduce_fusion
  51.7 1.2 fusion.43
  53.3 8.4 %all-gather.5.cloned.1.call-done = bf16[4,16,1536,16]{2,3,1,0:T(8,128)(2,1)} async-done(((bf16[4,1,1536,16]{2,3,1,0:T(8,128)(2,1)}), bf16[4,16,1536,16]{2,3,1,0:T(8,128)(2,1)}) %all-gather.5.cloned.1.call-update) | async-done | bytes 3145744 | tf_op jit(solution)/shard_map/all_gather | solution.py:82
  61.7 3.2 fusion.93
  64.9 0.4 fusion.88
  65.6 1.1 convolution_add_fusion.3
  66.7 1.1 copy.56
  67.8 0.7 pad_maximum_fusion
  68.8 1.6 fusion.86
  70.3 35.7 %all-gather.9.cloned.1.call-done = bf16[2,16,16,1536]{3,2,1,0:T(8,128)(2,1)} async-done(((bf16[2,1,16,1536]{3,2,1,0:T(8,128)(2,1)}), bf16[2,16,16,1536]{3,2,1,0:T(8,128)(2,1)}) %all-gather.9.cloned.1.call-update) | async-done | bytes 1572880 | tf_op jit(solution)/shard_map/all_gather | solution.py:83
  106.0 1.4 convolution_bitcast_fusion.1
  107.4 3.2 convolution_add_fusion.1
  110.9 1.6 fusion.84
  112.8 2.5 fusion.33
  115.3 16.3 %all-gather.7.cloned.1.call-done = bf16[1024,512]{0,1:T(8,128)(2,1)} async-done(((bf16[128,512]{0,1:T(8,128)(2,1)}), bf16[1024,512]{0,1:T(8,128)(2,1)}) %all-gather.7.cloned.1.call-update) | async-done | bytes 1048592 | tf_op jit(solution)/shard_map/all_gather | solution.py:113
  131.6 3.1 fusion
  134.8 4.5 copy-done.2
  139.4 3.0 fusion.2
  142.4 15.8 %all-gather.11.cloned.1.call-done = bf16[1024,512]{1,0:T(8,128)(2,1)} async-done(((bf16[128,512]{1,0:T(8,128)(2,1)}), bf16[1024,512]{1,0:T(8,128)(2,1)}) %all-gather.11.cloned.1.call-update) | async-done | bytes 1048592 | tf_op jit(solution)/shard_map/all_gather | solution.py:114
  158.2 2.3 copy.58
  160.5 8.1 %fusion.40 = bf16[128,8,3,64]{0,3,2,1:T(8,128)(2,1)S(1)} fusion(bf16[1024,8,64,1]{0,2,3,1:T(8,128)(2,1)} %bitcast.215, f32[8,1024,128,3]{2,1,3,0:T(8,128)} %copy-done.2, f32[8,3,128]{2,1,0:T(4,128)S(1)} %broadcast_maximum_fusion, pred[128,1024]{0,1:T(8,128)(4,1)S(1)} %fusion.51, f32[128,8,3]{0,2,1:T(4,128)S(1)} %bitcast.233), kind=kOutput, calls=%fused_computation.49 | convolution fusion | flops 418775040 | bytes 14180352 | tf_op jit(solution)/shard_map/ukoe,euh->ukoh/dot_general | solution.py:132
  168.5 0.4 fusion.95
  169.2 3.3 multiply_reduce_fusion
  172.7 11.9 %gather_fusion = bf16[3200,1536]{1,0:T(8,128)(2,1)} fusion(bf16[129,1536]{1,0:T(8,128)(2,1)S(1)} %concatenate.20, s32[4096]{0:T(1024)S(1)} %pad_clamp_fusion), kind=kCustom, calls=%fused_computation | custom fusion | bytes 19673600 | tf_op jit(solution)/shard_map/gather | solution.py:166
  184.5 117.5 %all_to_all.10 = bf16[16,5,40,1536]{3,2,1,0:T(8,128)(2,1)S(1)} all-to-all(bf16[16,5,40,1536]{3,2,1,0:T(8,128)(2,1)} %bitcast.208), channel_id=1, replica_groups=mesh['seq'=8,'grp'=16] {'grp'}, dimensions={0} | all-to-all | bytes 19660800 | tf_op jit(solution)/shard_map/all_to_all | solution.py:169
  302.1 3.8 copy-done.3
  305.8 4.6 fusion.6
  310.5 13.4 %fusion.1 = bf16[16,5,40,1536]{3,2,0,1:T(8,128)(2,1)} fusion(bf16[5,256,1536]{2,1,0:T(8,128)(2,1)} %param.35, f32[5,16,40,256]{3,2,1,0:T(8,128)} %fusion.6, bf16[5,1536,256]{2,1,0:T(8,128)(2,1)} %param.34, bf16[16,5,40,1536]{3,2,1,0:T(8,128)(2,1)} %copy-done.3), kind=kOutput, calls=%fused_computation.8 | convolution fusion | flops 5042995200 | bytes 30801920 | tf_op jit(solution)/shard_map/nlcf,lfd->nlcd/dot_general | solution.py:175
  323.9 8.3 %copy.70 = bf16[16,5,40,1536]{3,2,1,0:T(8,128)(2,1)} copy(bf16[16,5,40,1536]{3,2,0,1:T(8,128)(2,1)} %fusion.1) | data formatting | bytes 19660800 | tf_op jit(solution)/shard_map/convert_element_type | solution.py:177
  332.2 4.9 all-to-all-start.1
  337.1 0.3 compare_select_fusion
  338.2 141.3 %all-to-all-done.1 = bf16[16,5,40,1536]{3,2,1,0:T(8,128)(2,1)} async-done(((bf16[16,5,40,1536]{3,2,1,0:T(8,128)(2,1)}), bf16[16,5,40,1536]{3,2,1,0:T(8,128)(2,1)}, u32[]{:S(2)}, u32[]{:S(2)}) %all-to-all-start.1) | async-done | bytes 9830432 | tf_op jit(solution)/shard_map/all_to_all | solution.py:178
  479.5 18.3 %gather_fusion.1 = bf16[2048,1536]{1,0:T(8,128)(2,1)} fusion(bf16[3200,1536]{1,0:T(8,128)(2,1)} %bitcast.65, s32[2048]{0:T(1024)S(1)} %broadcast_clamp_fusion), kind=kCustom, calls=%fused_computation.1 | custom fusion | bytes 12591104 | tf_op jit(solution)/shard_map/gather | solution.py:183
  497.8 9.2 %convert_reduce_fusion = f32[128,1536]{1,0:T(8,128)S(1)} fusion(bf16[128,16,1536]{2,1,0:T(8,128)(2,1)} %bitcast.209, f32[128,16]{1,0:T(8,128)S(1)} %copy.62, s32[128,16]{1,0:T(8,128)S(1)} %copy.61), kind=kOutput, calls=%fused_computation.4 | convolution fusion | flops 613285888 | bytes 7094272 | tf_op jit(solution)/shard_map/tkg,tkd->tgd/dot_general | solution.py:189
  507.6 66.9 %all-reduce.2 = bf16[16,3,1536]{2,1,0:T(4,128)(2,1)S(1)} all-reduce(f32[16,3,1536]{2,1,0:T(4,128)S(1)} %broadcast_multiply_fusion), channel_id=1, replica_groups=mesh['seq'=8,'grp'=16] {'seq','grp'}, use_global_device_ids=true, to_apply=%region_15.16 | all-reduce | flops 73728 | bytes 442368 | tf_op jit(solution)/shard_map/psum | solution.py:200
  574.7 1.7 fusion.94
  576.4 64.0 %pmax.7 = f32[48]{0:T(128)S(1)} all-reduce(f32[48]{0:T(128)S(1)} %get-tuple-element.22), channel_id=1, replica_groups=mesh['seq'=8,'grp'=16] {'seq','grp'}, use_global_device_ids=true, to_apply=%region_17.18 | all-reduce | flops 48 | bytes 384 | tf_op jit(solution)/shard_map/pmax | solution.py:203
  640.6 62.6 %psum.15 = f32[48]{0:T(128)S(1)} all-reduce(f32[48]{0:T(128)S(1)} %exponential_reduce_fusion), channel_id=1, replica_groups=mesh['seq'=8,'grp'=16] {'seq','grp'}, use_global_device_ids=true, to_apply=%region_19.20 | all-reduce | flops 48 | bytes 384 | tf_op jit(solution)/shard_map/psum | solution.py:204
  703.2 0.7 broadcast_subtract_fusion
  (86 shorter events, 4.9 us)
Async XLA Ops:
  7.2 58.4 %copy-start = (bf16[1536,512]{1,0:T(8,128)(2,1)S(1)}, bf16[1536,512]{1,0:T(8,128)(2,1)}, u32[]{:S(2)}) copy-start(bf16[1536,512]{1,0:T(8,128)(2,1)} %param.26) | copy-start | bytes 4718596
  7.2 57.7 %copy-start.4 = (bf16[1,128,1536]{2,1,0:T(8,128)(2,1)S(1)}, bf16[1,128,1536]{2,1,0:T(8,128)(2,1)}, u32[]{:S(2)}) copy-start(bf16[1,128,1536]{2,1,0:T(8,128)(2,1)} %param.19) | copy-start | bytes 1179652
  7.2 57.7 %copy-start.7 = (f32[1536]{0:T(1024)S(1)}, f32[1536]{0:T(1024)}, u32[]{:S(2)}) copy-start(f32[1536]{0:T(1024)} %param.24) | copy-start | bytes 18436
  7.2 54.5 %all-gather.5.cloned.1.call-start = ((), (), s32[]{:S(2)}) async-start(), calls=%async_computation.2 | async-start | bytes 3342336 | tf_op jit(solution)/shard_map/all_gather | solution.py:82
  7.9 98.1 %all-gather.9.cloned.1.call-start = ((), (), s32[]{:S(2)}) async-start(), calls=%async_computation.4 | async-start | bytes 1671168 | tf_op jit(solution)/shard_map/all_gather | solution.py:83
  8.7 122.9 %all-gather.7.cloned.1.call-start = ((), (), s32[]{:S(2)}) async-start(), calls=%async_computation.3 | async-start | bytes 1179648 | tf_op jit(solution)/shard_map/all_gather | solution.py:113
  68.5 89.7 %all-gather.11.cloned.1.call-start = ((), (), s32[]{:S(2)}) async-start(), calls=%async_computation.5 | async-start | bytes 1179648 | tf_op jit(solution)/shard_map/all_gather | solution.py:114
  134.8 4.6 copy-start.2
  160.5 8.4 %copy-start.5 = (bf16[2,16,16,1536]{3,2,1,0:T(8,128)(2,1)S(1)}, bf16[2,16,16,1536]{3,2,1,0:T(8,128)(2,1)}, u32[]{:S(2)}) copy-start(bf16[2,16,16,1536]{3,2,1,0:T(8,128)(2,1)} %all-gather.9.cloned.1.call-done) | copy-start | bytes 4718596
  168.5 4.0 copy-start.8
  184.5 121.3 %copy-start.11 = (bf16[5,1536,256]{2,1,0:T(8,128)(2,1)S(1)}, bf16[5,1536,256]{2,1,0:T(8,128)(2,1)}, u32[]{:S(2)}) copy-start(bf16[5,1536,256]{2,1,0:T(8,128)(2,1)} %param.33) | copy-start | bytes 11796484
  302.1 3.8 copy-start.3
  332.2 5.8 copy-start.10
  332.2 147.3 %all-to-all-start.1 = ((bf16[16,5,40,1536]{3,2,1,0:T(8,128)(2,1)}), bf16[16,5,40,1536]{3,2,1,0:T(8,128)(2,1)}, u32[]{:S(2)}, u32[]{:S(2)}) async-start(bf16[16,5,40,1536]{3,2,1,0:T(8,128)(2,1)} %copy.70), calls=%async_computation.1 | async-start | bytes 19660800 | tf_op jit(solution)/shard_map/all_to_all | solution.py:178
  497.8 206.1 %copy-start.1 = (bf16[1536,512]{1,0:T(8,128)(2,1)S(1)}, bf16[1536,512]{1,0:T(8,128)(2,1)}, u32[]{:S(2)}) copy-start(bf16[1536,512]{1,0:T(8,128)(2,1)} %param.26) | copy-start | bytes 4718596
  497.8 9.6 %copy-start.9 = (f32[1536]{0:T(1024)S(1)}, f32[1536]{0:T(1024)}, u32[]{:S(2)}) copy-start(f32[1536]{0:T(1024)} %param.36) | copy-start | bytes 18436
  507.1 196.8 %copy-start.6 = (bf16[128,1536]{1,0:T(8,128)(2,1)}, bf16[128,1536]{1,0:T(8,128)(2,1)S(1)}, u32[]{:S(2)}) copy-start(bf16[128,1536]{1,0:T(8,128)(2,1)S(1)} %add_convert_fusion) | copy-start | bytes 1179652
Sparse Core Ops, SparseCore 0:
  10.2 51.4 all-gather.4
  63.8 42.1 all-gather.8
  107.7 23.8 all-gather.6
  133.8 24.3 all-gather.10
where the time goes:
time: 712 us; the launch traced here: 710 us
  blocking collectives  333 us (47%)
  waiting for transfers between devices  219 us (31%)
  local copies, waits for them, and re-layouts  60.3 us (8%)
  matrix products  56.6 us (8%)
  other arithmetic  21.7 us (3%)
  between operations  14.3 us (2%)
    all_to_all x1, waiting for transfers between devices, body(): lax.all_to_all(halves, 'grp', split_axis=0, concat_axis=0, tiled=True)  141 us
    all_to_all x1, blocking collectives, body(): lax.all_to_all(outgoing, 'grp', split_axis=0, concat_axis=0, tiled=True)  118 us
    psum x1, blocking collectives, body(): gathered = lax.psum(spread, ('seq', 'grp'))  66.9 us
    pmax x1, blocking collectives, body(): global_max = lax.pmax(jnp.max(logits, axis=1), ('seq', 'grp'))  64 us
    psum x1, blocking collectives, body(): lax.psum(jnp.sum(jnp.exp(logits - global_max[:, None]), axis=1), ('seq',...  62.6 us
    all_gather x1, waiting for transfers between devices, body(): lax.all_gather(adapter_up_query_output, 'grp', axis=1, tiled=True)  35.7 us
    all_gather x1, blocking collectives, body(): lax.all_gather(adapter_up_key_value, 'grp', axis=1, tiled=True)  22.3 us
    gather x1, local copies, waits for them, and re-layouts, body(): returned[pick_index].astype(jnp.float32)  18.3 us
  transfers between devices with their start and end apart: 5, of which 5 were waited for; matrix products, arithmetic and copies ran while one was open for 7% of the time, Pallas kernels for 0%

commit v1 on v0

--- a/solution.py
+++ b/solution.py
@@ -111,7 +111,16 @@
     ).astype(jnp.bfloat16)
     running_max = jnp.full((KV_HEADS, ratio, tok_count), MASKED, jnp.float32)
     key_part = lax.all_gather(key_matrix, "seq", axis=0, tiled=True)
-    value_part = lax.all_gather(value_matrix, "seq", axis=0, tiled=True)
+    q_n = lax.axis_size("seq")
+    by_place = [value_matrix]
+    for k0 in range(q_n - 1):
+        piece_next = lax.ppermute(
+            by_place[-1], "seq", [(idx, (idx + 1) % q_n) for idx in range(q_n)]
+        )
+        by_place.append(piece_next)
+    a_now = jnp.concatenate(by_place[::-1], axis=0)
+    all_values = lax.axis_index("seq")
+    value_part = jnp.roll(a_now, (all_values + 1) * value_matrix.shape[0], 0)
     key_count = key_part.shape[0]
     key_index = jnp.arange(key_count, dtype=jnp.int32)
     key_doc, _, _ = doc_layout(prompt_lens, key_index)

time: 712 us -> 683 us (0.959)
  waiting for transfers between devices: 219 us -> 186 us
  starting transfers between devices: 5.27 us -> 19.1 us
  matrix products: 56.6 us -> 45.3 us
    all_gather x1, waiting for transfers between devices: 35.7 us -> 19.8 us  [body(): lax.all_gather(adapter_up_query_output, 'grp', axis=1, tiled=True)]
    all_gather x1 -> x0, waiting for transfers between devices: 15.8 us -> none  [body(): value_part = lax.all_gather(value_matrix, 'seq', axis=0, tiled=True)]
    ppermute x0 -> x7, starting transfers between devices: none -> 14.2 us  [body(): lax.ppermute(by_place[-1], 'seq', [(idx, (idx + 1) % q_n) for idx in rang...]
    ppermute x0 -> x7, waiting for transfers between devices: none -> 8.49 us  [body(): lax.ppermute(by_place[-1], 'seq', [(idx, (idx + 1) % q_n) for idx in rang...]
    all_gather x1, waiting for transfers between devices: 16.3 us -> 9.15 us  [body(): key_part = lax.all_gather(key_matrix, 'seq', axis=0, tiled=True)]
  transfers between devices with their start and end apart: 5 -> 11, of which waited for: 5 -> 9; matrix products, arithmetic and copies ran while one was open for 7% -> 6% of each run, Pallas kernels for 0% -> 0%
where the time goes in v1:
time: 683 us; the launch traced here: 682 us
  blocking collectives  334 us (49%)
  waiting for transfers between devices  186 us (27%)
  local copies, waits for them, and re-layouts  57.9 us (8%)
  matrix products  45.3 us (7%)
  other arithmetic  24.9 us (4%)
  starting transfers between devices  19.1 us (3%)
  between operations  14.6 us (2%)
    all_to_all x1, waiting for transfers between devices, body(): lax.all_to_all(halves, 'grp', split_axis=0, concat_axis=0, tiled=True)  141 us
    all_to_all x1, blocking collectives, body(): lax.all_to_all(outgoing, 'grp', split_axis=0, concat_axis=0, tiled=True)  118 us
    psum x1, blocking collectives, body(): gathered = lax.psum(spread, ('seq', 'grp'))  68.2 us
    psum x1, blocking collectives, body(): lax.psum(jnp.sum(jnp.exp(logits - global_max[:, None]), axis=1), ('seq',...  64 us
    pmax x1, blocking collectives, body(): global_max = lax.pmax(jnp.max(logits, axis=1), ('seq', 'grp'))  62.5 us
    all_gather x1, blocking collectives, body(): lax.all_gather(adapter_up_key_value, 'grp', axis=1, tiled=True)  22 us
    all_gather x1, waiting for transfers between devices, body(): lax.all_gather(adapter_up_query_output, 'grp', axis=1, tiled=True)  19.8 us
    gather x1, local copies, waits for them, and re-layouts, body(): returned[pick_index].astype(jnp.float32)  18.3 us
  transfers between devices with their start and end apart: 11, of which 9 were waited for; matrix products, arithmetic and copies ran while one was open for 6% of the time, Pallas kernels for 0%

profile of v1, /device:TPU:1, one launch (start us, length us, event | category | flops | bytes accessed | tf_op | source)
XLA Modules:
  0.0 682.1 jit_solution(3298845460203546452)
XLA Ops:
  9.7 1.3 multiply_bitcast_fusion
  13.4 1.2 fusion.43
  15.2 22.0 %all_gather.13 = bf16[2,16,16,512]{3,2,1,0:T(8,128)(2,1)S(1)} all-gather(bf16[2,1,16,512]{3,2,1,0:T(8,128)(2,1)} %param.31), channel_id=1, replica_groups=mesh['seq'=8,'grp'=16] {'grp'}, dimensions={1}, use_global_device_ids=true | all-gather | bytes 557056 | tf_op jit(solution)/shard_map/all_gather | solution.py:84
  37.2 11.3 %reduce-window.11 = s32[40,8,128]{2,1,0:T(8,128)S(1)} reduce-window(s32[40,8,128]{2,1,0:T(8,128)S(1)} %fusion.60, s32[]{:T(128)} %constant.87.clone.1), window={size=1x1x128 pad=0_0x0_0x127_0}, to_apply=%region_9.10 | reduce-window | flops 5201920 | bytes 327684 | tf_op jit(solution)/shard_map/reduce-window.1
  49.3 4.5 scatter_custom_fusion
  55.6 5.9 all-gather.4.cloned.1.call-done
  61.5 2.9 fusion.93
  64.5 1.2 fusion.84
  66.4 2.1 collective-permute-start
  69.2 1.3 collective-permute-done
  70.5 2.4 collective-permute-start.1
  73.5 1.4 collective-permute-done.1
  74.9 2.4 collective-permute-start.2
  78.1 1.4 collective-permute-done.2
  79.5 2.2 collective-permute-start.3
  82.2 2.9 collective-permute-done.3
  85.2 1.0 collective-permute-start.4
  86.2 19.8 %all-gather.8.cloned.1.call-done = bf16[2,16,16,1536]{3,2,1,0:T(8,128)(2,1)} async-done(((bf16[2,1,16,1536]{3,2,1,0:T(8,128)(2,1)}), bf16[2,16,16,1536]{3,2,1,0:T(8,128)(2,1)}) %all-gather.8.cloned.1.call-update) | async-done | bytes 1572880 | tf_op jit(solution)/shard_map/all_gather | solution.py:83
  105.9 1.4 convolution_bitcast_fusion.1
  107.4 2.7 collective-permute-start.5
  110.1 3.2 convolution_add_fusion.1
  113.6 1.2 collective-permute-start.6
  114.8 0.8 subtract_convert_fusion
  115.7 1.4 collective-permute-done.6
  117.1 0.9 constant_dynamic-update-slice_fusion.14
  118.0 0.9 constant_dynamic-update-slice_fusion.13
  119.1 0.9 constant_dynamic-update-slice_fusion.6
  120.0 0.9 constant_dynamic-update-slice_fusion.5
  121.1 1.3 copy.57
  122.4 9.2 %all-gather.6.cloned.1.call-done = bf16[1024,512]{0,1:T(8,128)(2,1)} async-done(((bf16[128,512]{0,1:T(8,128)(2,1)}), bf16[1024,512]{0,1:T(8,128)(2,1)}) %all-gather.6.cloned.1.call-update) | async-done | bytes 1048592 | tf_op jit(solution)/shard_map/all_gather | solution.py:113
  131.6 3.1 fusion
  134.7 3.0 fusion.2
  137.8 3.5 fusion.40
  142.0 0.9 multiply_reduce_fusion
  143.2 11.9 %gather_fusion = bf16[3200,1536]{1,0:T(8,128)(2,1)} fusion(bf16[129,1536]{1,0:T(8,128)(2,1)S(1)} %concatenate.27, s32[4096]{0:T(1024)S(1)} %copy-done.13), kind=kCustom, calls=%fused_computation | custom fusion | bytes 19673600 | tf_op jit(solution)/shard_map/gather | solution.py:175
  155.1 117.5 %all_to_all.10 = bf16[16,5,40,1536]{3,2,1,0:T(8,128)(2,1)S(1)} all-to-all(bf16[16,5,40,1536]{3,2,1,0:T(8,128)(2,1)} %bitcast.208), channel_id=1, replica_groups=mesh['seq'=8,'grp'=16] {'grp'}, dimensions={0} | all-to-all | bytes 19660800 | tf_op jit(solution)/shard_map/all_to_all | solution.py:178
  272.6 3.8 copy-done.2
  276.4 4.7 fusion.6
  281.1 13.3 %fusion.1 = bf16[16,5,40,1536]{3,2,0,1:T(8,128)(2,1)} fusion(bf16[5,256,1536]{2,1,0:T(8,128)(2,1)} %param.35, f32[5,16,40,256]{3,2,1,0:T(8,128)} %fusion.6, bf16[5,1536,256]{2,1,0:T(8,128)(2,1)} %param.34, bf16[16,5,40,1536]{3,2,1,0:T(8,128)(2,1)} %copy-done.2), kind=kOutput, calls=%fused_computation.8 | convolution fusion | flops 5042995200 | bytes 30801920 | tf_op jit(solution)/shard_map/nlcf,lfd->nlcd/dot_general | solution.py:184
  294.4 8.3 %copy.69 = bf16[16,5,40,1536]{3,2,1,0:T(8,128)(2,1)} copy(bf16[16,5,40,1536]{3,2,0,1:T(8,128)(2,1)} %fusion.1) | data formatting | bytes 19660800 | tf_op jit(solution)/shard_map/convert_element_type | solution.py:186
  302.6 4.8 all-to-all-start.1
  308.6 141.3 %all-to-all-done.1 = bf16[16,5,40,1536]{3,2,1,0:T(8,128)(2,1)} async-done(((bf16[16,5,40,1536]{3,2,1,0:T(8,128)(2,1)}), bf16[16,5,40,1536]{3,2,1,0:T(8,128)(2,1)}, u32[]{:S(2)}, u32[]{:S(2)}) %all-to-all-start.1) | async-done | bytes 9830432 | tf_op jit(solution)/shard_map/all_to_all | solution.py:187
  449.9 18.3 %gather_fusion.1 = bf16[2048,1536]{1,0:T(8,128)(2,1)} fusion(bf16[3200,1536]{1,0:T(8,128)(2,1)} %bitcast.65, s32[2048]{0:T(1024)S(1)} %broadcast_clamp_fusion), kind=kCustom, calls=%fused_computation.1 | custom fusion | bytes 12591104 | tf_op jit(solution)/shard_map/gather | solution.py:192
  468.2 9.2 %convert_reduce_fusion = f32[128,1536]{1,0:T(8,128)S(1)} fusion(bf16[128,16,1536]{2,1,0:T(8,128)(2,1)} %bitcast.209, f32[128,16]{1,0:T(8,128)S(1)} %copy.61, s32[128,16]{1,0:T(8,128)S(1)} %copy.60), kind=kOutput, calls=%fused_computation.4 | convolution fusion | flops 613285888 | bytes 7094272 | tf_op jit(solution)/shard_map/tkg,tkd->tgd/dot_general | solution.py:198
  478.1 68.2 %all-reduce.2 = bf16[16,3,1536]{2,1,0:T(4,128)(2,1)S(1)} all-reduce(f32[16,3,1536]{2,1,0:T(4,128)S(1)} %broadcast_multiply_fusion), channel_id=1, replica_groups=mesh['seq'=8,'grp'=16] {'seq','grp'}, use_global_device_ids=true, to_apply=%region_15.16 | all-reduce | flops 73728 | bytes 442368 | tf_op jit(solution)/shard_map/psum | solution.py:209
  546.4 1.7 fusion.94
  548.1 62.5 %pmax.7 = f32[48]{0:T(128)S(1)} all-reduce(f32[48]{0:T(128)S(1)} %get-tuple-element.22), channel_id=1, replica_groups=mesh['seq'=8,'grp'=16] {'seq','grp'}, use_global_device_ids=true, to_apply=%region_17.18 | all-reduce | flops 48 | bytes 384 | tf_op jit(solution)/shard_map/pmax | solution.py:212
  610.8 64.0 %psum.15 = f32[48]{0:T(128)S(1)} all-reduce(f32[48]{0:T(128)S(1)} %exponential_reduce_fusion), channel_id=1, replica_groups=mesh['seq'=8,'grp'=16] {'seq','grp'}, use_global_device_ids=true, to_apply=%region_19.20 | all-reduce | flops 48 | bytes 384 | tf_op jit(solution)/shard_map/psum | solution.py:213
  (159 shorter events, 15.0 us)
Async XLA Ops:
  7.2 58.8 %copy-start = (bf16[1536,512]{1,0:T(8,128)(2,1)S(1)}, bf16[1536,512]{1,0:T(8,128)(2,1)}, u32[]{:S(2)}) copy-start(bf16[1536,512]{1,0:T(8,128)(2,1)} %param.27) | copy-start | bytes 4718596
  7.2 54.3 %all-gather.4.cloned.1.call-start = ((), (), s32[]{:S(2)}) async-start(), calls=%async_computation.2 | async-start | bytes 3342336 | tf_op jit(solution)/shard_map/all_gather | solution.py:82
  7.9 98.0 %all-gather.8.cloned.1.call-start = ((), (), s32[]{:S(2)}) async-start(), calls=%async_computation.4 | async-start | bytes 1671168 | tf_op jit(solution)/shard_map/all_gather | solution.py:83
  8.7 122.9 %all-gather.6.cloned.1.call-start = ((), (), s32[]{:S(2)}) async-start(), calls=%async_computation.3 | async-start | bytes 1179648 | tf_op jit(solution)/shard_map/all_gather | solution.py:113
  9.7 44.1 %copy-start.19 = (s32[1024]{0:T(1024)}, s32[1024]{0:T(1024)S(1)}, u32[]{:S(2)}) copy-start(s32[1024]{0:T(1024)S(1)} %broadcast_in_dim_reshape_squeeze.2) | copy-start | bytes 12292
  11.0 53.5 %copy-start.27 = (s32[128]{0:T(128)}, s32[128]{0:T(128)S(1)}, u32[]{:S(2)}) copy-start(s32[128]{0:T(128)S(1)} %iota_add_fusion) | copy-start | bytes 1540
  11.8 0.8 copy-start.29
  49.2 4.5 copy-start.17
  53.9 10.6 %copy-start.3 = (bf16[1,128,1536]{2,1,0:T(8,128)(2,1)S(1)}, bf16[1,128,1536]{2,1,0:T(8,128)(2,1)}, u32[]{:S(2)}) copy-start(bf16[1,128,1536]{2,1,0:T(8,128)(2,1)} %param.19) | copy-start | bytes 1179652
  53.9 10.6 %copy-start.16 = (f32[1536]{0:T(1024)S(1)}, f32[1536]{0:T(1024)}, u32[]{:S(2)}) copy-start(f32[1536]{0:T(1024)} %param.24) | copy-start | bytes 18436
  61.5 4.4 copy-start.24
  64.5 8.5 %copy-start.4 = (bf16[1536,512]{1,0:T(8,128)(2,1)S(1)}, bf16[1536,512]{1,0:T(8,128)(2,1)}, u32[]{:S(2)}) copy-start(bf16[1536,512]{1,0:T(8,128)(2,1)} %param.26) | copy-start | bytes 4718596
  66.4 11.0 %copy-start.14 = (f32[128,32]{0,1:T(8,128)S(1)}, f32[128,32]{0,1:T(8,128)}, u32[]{:S(2)}) copy-start(f32[128,32]{0,1:T(8,128)} %get-tuple-element.14) | copy-start | bytes 49156
  66.4 11.0 %copy-start.15 = (f32[128,32]{0,1:T(8,128)S(1)}, f32[128,32]{0,1:T(8,128)}, u32[]{:S(2)}) copy-start(f32[128,32]{0,1:T(8,128)} %get-tuple-element.15) | copy-start | bytes 49156
  66.4 15.4 %copy-start.8 = (bf16[1,16,1536,16]{2,3,1,0:T(8,128)(2,1)S(1)}, bf16[1,16,1536,16]{2,3,1,0:T(8,128)(2,1)}, u32[]{:S(2)}) copy-start(bf16[1,16,1536,16]{2,3,1,0:T(8,128)(2,1)} %get-tuple-element.4) | copy-start | bytes 2359300
  66.4 15.3 %copy-start.25 = (f32[128]{0:T(128)S(1)}, f32[128]{0:T(128)}, u32[]{:S(2)}) copy-start(f32[128]{0:T(128)} %add_rsqrt_fusion.2) | copy-start | bytes 1540
  66.4 4.1 collective-permute-start
  70.5 36.8 %copy-start.9 = (bf16[128,512]{1,0:T(8,128)(2,1)}, bf16[128,512]{1,0:T(8,128)(2,1)S(1)}, u32[]{:S(2)}) copy-start(bf16[128,512]{1,0:T(8,128)(2,1)S(1)} %collective-permute-done) | copy-start | bytes 393220
  70.5 4.4 collective-permute-start.1
  74.9 32.5 %copy-start.11 = (bf16[128,512]{1,0:T(8,128)(2,1)}, bf16[128,512]{1,0:T(8,128)(2,1)S(1)}, u32[]{:S(2)}) copy-start(bf16[128,512]{1,0:T(8,128)(2,1)S(1)} %collective-permute-done.1) | copy-start | bytes 393220
  74.9 4.6 collective-permute-start.2
  79.5 5.6 collective-permute-start.3
  85.2 22.2 %collective-permute-start.4 = (bf16[128,512]{1,0:T(8,128)(2,1)S(1)}, bf16[128,512]{1,0:T(8,128)(2,1)}, u32[]{:S(2)}, u32[]{:S(2)}) collective-permute-start(bf16[128,512]{1,0:T(8,128)(2,1)S(1)} %collective-permute-done.3), channel_id=1, source_target_pairs={{0,16},{16,32},{32,48},{48,64},{64,80},{80,96},{96,112},{112,0},{1... | collective-permute-start | bytes 393224 | tf_op jit(solution)/shard_map/ppermute | solution.py:117
  107.4 6.2 collective-permute-start.5
  113.3 5.7 copy-start.12
  113.3 5.7 copy-start.10
  113.6 3.5 collective-permute-start.6
  134.7 3.1 copy-start.7
  137.8 4.2 slice-start
  137.8 3.9 copy-start.5
  137.8 4.2 slice-start.1
  142.0 1.0 copy-start.22
  142.0 1.1 copy-start.13
  155.1 121.3 %copy-start.31 = (bf16[5,1536,256]{2,1,0:T(8,128)(2,1)S(1)}, bf16[5,1536,256]{2,1,0:T(8,128)(2,1)}, u32[]{:S(2)}) copy-start(bf16[5,1536,256]{2,1,0:T(8,128)(2,1)} %param.33) | copy-start | bytes 11796484
  272.6 3.8 copy-start.2
  302.6 4.8 copy-start.20
  302.6 4.9 copy-start.18
  302.6 5.6 copy-start.21
  302.6 5.8 copy-start.26
  302.6 5.9 copy-start.30
  302.6 147.2 %all-to-all-start.1 = ((bf16[16,5,40,1536]{3,2,1,0:T(8,128)(2,1)}), bf16[16,5,40,1536]{3,2,1,0:T(8,128)(2,1)}, u32[]{:S(2)}, u32[]{:S(2)}) async-start(bf16[16,5,40,1536]{3,2,1,0:T(8,128)(2,1)} %copy.69), calls=%async_computation.1 | async-start | bytes 19660800 | tf_op jit(solution)/shard_map/all_to_all | solution.py:187
  468.2 9.3 %copy-start.28 = (s32[128]{0:T(128)S(1)}, s32[128]{0:T(128)}, u32[]{:S(2)}) copy-start(s32[128]{0:T(128)} %copy-done.27) | copy-start | bytes 1540
  468.2 9.6 %copy-start.23 = (f32[1536]{0:T(1024)S(1)}, f32[1536]{0:T(1024)}, u32[]{:S(2)}) copy-start(f32[1536]{0:T(1024)} %param.36) | copy-start | bytes 18436
  468.2 207.3 %copy-start.1 = (bf16[1536,512]{1,0:T(8,128)(2,1)S(1)}, bf16[1536,512]{1,0:T(8,128)(2,1)}, u32[]{:S(2)}) copy-start(bf16[1536,512]{1,0:T(8,128)(2,1)} %param.27) | copy-start | bytes 4718596
  477.5 198.1 %copy-start.6 = (bf16[128,1536]{1,0:T(8,128)(2,1)}, bf16[128,1536]{1,0:T(8,128)(2,1)S(1)}, u32[]{:S(2)}) copy-start(bf16[128,1536]{1,0:T(8,128)(2,1)S(1)} %add_convert_fusion) | copy-start | bytes 1179652
Sparse Core Ops, SparseCore 0:
  10.2 51.3 all-gather.3
  63.7 42.2 all-gather.7
  107.6 23.8 all-gather.5
